TPU v7x, 512 devices: a whole 4x8x8 slice. The times are simulated.
512 devices in a mesh: req: 32 (over y_hi, x, core), tp: 16 (over z, y_lo).
Axes of the slice: x: 4, y: 8 (y_hi: 4, y_lo: 2; y = y_hi * 2 + y_lo), z: 8, core: 2. Of those that a mesh axis runs over, the one named last changes fastest.
Arguments:
- hidden: bfloat16 [32, 256, 4096], P('req', None, 'tp'), may hold values from -6 to 6
- norm_gain: bfloat16 [4096], P('tp'), may hold values from 0.5 to 1.5
- w_query: bfloat16 [4096, 2048], P(None, 'tp'), may hold values from -0.09375 to 0.09375
- w_key: bfloat16 [4096, 2048], P(None, 'tp'), may hold values from -0.09375 to 0.09375
- w_value: bfloat16 [4096, 2048], P(None, 'tp'), may hold values from -0.09375 to 0.09375
- w_out: bfloat16 [2048, 4096], P('tp'), may hold values from -0.5 to 0.5
- prefix_keys: bfloat16 [16384, 2048], P('req', 'tp'), may hold values from -1000 to 1000
- prefix_values: bfloat16 [16384, 2048], P('req', 'tp'), may hold values from -6 to 6
- lengths: int32 [32], P('req'), may hold values from 32 to 256, as said below
Outputs:
- attended: bfloat16 [32, 256, 4096], P('req', 'tp')
Inputs may be any that keep to these rules, and one draw needn't show every extreme that they name: `lengths`: every request has at least 32 suffix tokens; in every draw some request has exactly 256.
All inputs are finite; a program needn't handle non-finite values.
Results may differ from a plain program's by a relative error of at most 0.029.
Values may be sent and summed in bfloat16 or wider, within the bound.
A program may use at most 64 MiB of HBM per device.

v0:
```python
import jax
import jax.numpy as jnp
from jax import lax
from jax.sharding import PartitionSpec as P


def rotate(values, angles):
    half = values.shape[-1] // 2
    cosine = jnp.cos(angles)
    sine = jnp.sin(angles)
    first = values[..., :half]
    second = values[..., half:]
    return jnp.concatenate(
        [first * cosine - second * sine, second * cosine + first * sine], axis=-1
    )


def on_device(
    hidden, norm_gain, w_query, w_key, w_value, w_out, prefix_keys, prefix_values, lengths
):
    full, gain = (
        lax.all_gather(hidden, "tp", axis=2, tiled=True),
        lax.all_gather(norm_gain, "tp", axis=0, tiled=True),
    )
    x = full[0].astype(jnp.float32)
    slot = x.shape[0]
    head_dim = w_query.shape[1]
    groups = lax.axis_size("req")
    prefix = prefix_keys.shape[0] * groups
    normed = (
        x * lax.rsqrt(jnp.mean(x * x, axis=-1, keepdims=True) + 1e-05) * gain.astype(jnp.float32)
    ).astype(jnp.bfloat16)
    positions = (prefix + jnp.arange(slot)).astype(jnp.float32)
    freq = 10000.0 ** (-2.0 * jnp.arange(head_dim // 2).astype(jnp.float32) / head_dim)
    angles = positions[:, None] * freq[None, :]
    query = rotate(jnp.dot(normed, w_query, preferred_element_type=jnp.float32), angles).astype(
        jnp.bfloat16
    )
    key_new = rotate(jnp.dot(normed, w_key, preferred_element_type=jnp.float32), angles).astype(
        jnp.bfloat16
    )
    value_new = jnp.dot(normed, w_value, preferred_element_type=jnp.float32).astype(jnp.bfloat16)
    scale = 1.0 / head_dim**0.5
    causal = jnp.arange(slot)[:, None] >= jnp.arange(slot)[None, :]
    own_scores = jnp.einsum("sd,td->st", query, key_new, preferred_element_type=jnp.float32) * scale
    own_scores = jnp.where(causal, own_scores, -jnp.inf)
    top = jnp.max(own_scores, axis=-1)
    own_weights = jnp.where(causal, jnp.exp(own_scores - top[:, None]), 0.0).astype(jnp.bfloat16)
    total = jnp.sum(own_weights.astype(jnp.float32), axis=-1)
    acc = jnp.dot(own_weights, value_new, preferred_element_type=jnp.float32)
    run_total = total
    run_acc = acc
    keys = lax.all_gather(prefix_keys, "req", axis=0, tiled=True)
    values = lax.all_gather(prefix_values, "req", axis=0, tiled=True)
    scores = jnp.einsum("sd,pd->sp", query, keys, preferred_element_type=jnp.float32) * scale
    new_top = jnp.maximum(top, jnp.max(scores, axis=-1))
    fade = jnp.exp(top - new_top)
    weights = jnp.exp(scores - new_top[:, None]).astype(jnp.bfloat16)
    run_total = run_total * fade + jnp.sum(weights.astype(jnp.float32), axis=-1)
    run_acc = run_acc * fade[:, None] + jnp.dot(weights, values, preferred_element_type=jnp.float32)
    context = (run_acc / run_total[:, None]).astype(jnp.bfloat16)
    rows = slot // lax.axis_size("tp")
    summed = lax.psum_scatter(
        jnp.dot(context, w_out, preferred_element_type=jnp.float32).astype(jnp.bfloat16),
        "tp",
        scatter_dimension=0,
        tiled=True,
    ).astype(jnp.float32)
    index = lax.axis_index("tp") * rows + jnp.arange(rows)
    keep = index < lengths[0]
    return jnp.where(keep[:, None], summed, 0.0).astype(jnp.bfloat16)[None]


def solution(mesh):
    return jax.shard_map(
        on_device,
        mesh=mesh,
        in_specs=(
            P("req", None, "tp"),
            P("tp"),
            P(None, "tp"),
            P(None, "tp"),
            P(None, "tp"),
            P("tp", None),
            P("req", "tp"),
            P("req", "tp"),
            P("req"),
        ),
        out_specs=P("req", "tp", None),
        check_vma=False,
    )
```

profile of v0, /device:TPU:2, one launch (start us, length us, event | category | flops | bytes accessed | tf_op | source)
XLA Modules:
  0.0 325.4 jit_solution(8467891159178002061)
XLA Ops:
  6.5 0.0 copy-start
  6.5 0.0 all-gather.5.cloned.1.call-start
  6.5 0.7 all-gather.5.cloned.1.call-update
  7.3 0.0 all-gather.7.cloned.1.call-start
  7.3 0.7 all-gather.7.cloned.1.call-update
  8.0 0.0 all-gather.9.cloned.1.call-start
  8.1 0.7 all-gather.9.cloned.1.call-update
  8.7 0.0 reduce-scatter.2.cloned.1.call-start
  8.8 0.7 reshape.50
  9.5 39.7 %all-gather = bf16[16,1,256]{2,1,0:T(2,128)(2,1)S(1)} all-gather(bf16[1,1,256]{2,1,0:T(2,128)(2,1)S(1)} %reshape.50), channel_id=1, replica_groups=mesh['req'=32,'tp'=16] {'tp'}, dimensions={0}, use_global_device_ids=true | all-gather | bytes 8704 | tf_op jit(solution)/shard_map/all_gather | solution.py:23
  49.2 44.7 %all-gather.5.cloned.1.call-done = bf16[1,256,4096]{2,1,0:T(8,128)(2,1)} async-done(((bf16[1,256,256]{2,1,0:T(8,128)(2,1)}), bf16[1,256,4096]{2,1,0:T(8,128)(2,1)}) %all-gather.5.cloned.1.call-update) | async-done | bytes 2097168 | tf_op jit(solution)/shard_map/all_gather | solution.py:22
  93.9 2.2 fusion
  96.1 0.0 copy-start.3
  96.1 2.9 fusion.34
  99.0 0.0 copy-done.2
  99.0 0.0 copy-done.1
  99.0 1.0 fusion.36
  100.0 0.3 fusion.21
  100.4 0.2 fusion.38
  100.6 0.1 convert_reduce_fusion.1
  100.7 0.0 copy-done.3
  100.7 0.9 convolution_convert_fusion.1
  101.6 59.2 %all-gather.7.cloned.1.call-done = bf16[16384,128]{1,0:T(8,128)(2,1)} async-done(((bf16[512,128]{1,0:T(8,128)(2,1)}), bf16[16384,128]{1,0:T(8,128)(2,1)}) %all-gather.7.cloned.1.call-update) | async-done | bytes 4194320 | tf_op jit(solution)/shard_map/all_gather | solution.py:53
  160.7 4.6 %fusion.39 = (f32[256]{0:T(256)S(1)}, f32[256,16384]{1,0:T(8,128)S(1)}) fusion(bf16[16384,128]{1,0:T(8,128)(2,1)} %all-gather.7.cloned.1.call-done, bf16[256,64]{0,1:T(8,128)(2,1)S(1)} %get-tuple-element.13, bf16[256,64]{0,1:T(8,128)(2,1)S(1)} %get-tuple-element.14), kind=kOutput, calls=%fused_computation.57 | convolution fusion | flops 1082261248 | bytes 21038080 | tf_op jit(solution)/shard_map/sd,pd->sp/dot_general | solution.py:55
  165.4 5.4 %convert_reduce_fusion = (f32[256]{0:T(256)S(1)}, bf16[256,16384]{1,0:T(8,128)(2,1)}) fusion(f32[256,16384]{1,0:T(8,128)S(1)} %get-tuple-element.18, f32[256]{0:T(256)S(1)} %max.13), kind=kLoop, calls=%fused_computation.1 | loop fusion | flops 16776960 | bytes 25167872 | tf_op jit(solution)/shard_map/reduce_sum | solution.py:59
  170.8 56.6 %all-gather.9.cloned.1.call-done = bf16[16384,128]{1,0:T(8,128)(2,1)} async-done(((bf16[512,128]{1,0:T(8,128)(2,1)}), bf16[16384,128]{1,0:T(8,128)(2,1)}) %all-gather.9.cloned.1.call-update) | async-done | bytes 4194320 | tf_op jit(solution)/shard_map/all_gather | solution.py:54
  227.4 6.9 %fusion.40 = f32[256,128]{1,0:T(8,128)S(1)} fusion(bf16[256,16384]{1,0:T(8,128)(2,1)} %get-tuple-element.8, bf16[16384,128]{1,0:T(8,128)(2,1)} %all-gather.9.cloned.1.call-done), kind=kOutput, calls=%fused_computation.58 | convolution fusion | flops 1073741824 | bytes 12713984 | tf_op jit(solution)/shard_map/dot_general | solution.py:60
  234.3 0.0 copy-done
  234.3 2.2 convolution_convert_fusion
  236.5 0.0 reduce-scatter.2.cloned.1.call-update
  237.2 80.0 %reduce-scatter.2.cloned.1.call-done = bf16[16,4096]{1,0:T(8,128)(2,1)} async-done(((bf16[256,4096]{1,0:T(8,128)(2,1)}), bf16[16,4096]{1,0:T(8,128)(2,1)}) %reduce-scatter.2.cloned.1.call-update) | async-done | bytes 131088 | tf_op jit(solution)/shard_map/reduce_scatter | solution.py:63
  317.2 1.6 fusion.7
  (9 shorter events, 0.1 us)
Async XLA Ops:
  6.5 227.8 %copy-start = (bf16[128,4096]{1,0:T(8,128)(2,1)S(1)}, bf16[128,4096]{1,0:T(8,128)(2,1)}, u32[]{:S(2)}) copy-start(bf16[128,4096]{1,0:T(8,128)(2,1)} %param.14) | copy-start | bytes 3145732
  6.5 92.5 %copy-start.2 = (bf16[4096,128]{1,0:T(8,128)(2,1)S(1)}, bf16[4096,128]{1,0:T(8,128)(2,1)}, u32[]{:S(2)}) copy-start(bf16[4096,128]{1,0:T(8,128)(2,1)} %param.11) | copy-start | bytes 3145732
  6.5 87.3 %all-gather.5.cloned.1.call-start = ((), (), s32[]{:S(2)}) async-start(), calls=%async_computation.1 | async-start | bytes 2228224 | tf_op jit(solution)/shard_map/all_gather | solution.py:22
  7.3 153.5 %all-gather.7.cloned.1.call-start = ((), (), s32[]{:S(2)}) async-start(), calls=%async_computation.2 | async-start | bytes 4325376 | tf_op jit(solution)/shard_map/all_gather | solution.py:53
  8.0 219.4 %all-gather.9.cloned.1.call-start = ((), (), s32[]{:S(2)}) async-start(), calls=%async_computation.3 | async-start | bytes 4325376 | tf_op jit(solution)/shard_map/all_gather | solution.py:54
  8.7 308.4 %reduce-scatter.2.cloned.1.call-start = ((), (), s32[]{:S(2)}) async-start(), calls=%async_computation.4 | async-start | bytes 2228224 | tf_op jit(solution)/shard_map/reduce_scatter | solution.py:63
  93.9 5.2 %copy-start.1 = (bf16[1,256,4096]{2,1,0:T(8,128)(2,1)S(1)}, bf16[1,256,4096]{2,1,0:T(8,128)(2,1)}, u32[]{:S(2)}) copy-start(bf16[1,256,4096]{2,1,0:T(8,128)(2,1)} %all-gather.5.cloned.1.call-done) | copy-start | bytes 6291460
  96.1 4.6 %copy-start.3 = (bf16[4096,128]{1,0:T(8,128)(2,1)S(1)}, bf16[4096,128]{1,0:T(8,128)(2,1)}, u32[]{:S(2)}) copy-start(bf16[4096,128]{1,0:T(8,128)(2,1)} %param.13) | copy-start | bytes 3145732
Sparse Core Ops, SparseCore 0:
  9.3 84.4 all-gather.4
  97.0 63.7 all-gather.6
  163.9 63.4 all-gather.8
  236.7 80.4 reduce-scatter.1
where the time goes:
time: 326 us; the launch traced here: 325 us
  waiting for transfers between devices  243 us (75%)
  blocking collectives  39.7 us (12%)
  matrix products  18.7 us (6%)
  between operations  13.9 us (4%)
  other arithmetic  9.72 us (3%)
    reduce_scatter x1, waiting for transfers between devices, on_device(): lax.psum_scatter(jnp.dot(context, w_out, preferred_element_type=jnp.float...  80 us
    all_gather x1, waiting for transfers between devices, on_device(): keys = lax.all_gather(prefix_keys, 'req', axis=0, tiled=True)  59.2 us
    all_gather x1, waiting for transfers between devices, on_device(): values = lax.all_gather(prefix_values, 'req', axis=0, tiled=True)  56.6 us
    all_gather x1, waiting for transfers between devices, on_device(): lax.all_gather(hidden, 'tp', axis=2, tiled=True)  44.7 us
    all_gather x1, blocking collectives, on_device(): lax.all_gather(norm_gain, 'tp', axis=0, tiled=True)  39.7 us
    dot_general x1, matrix products, on_device(): jnp.dot(weights, values, preferred_element_type=jnp.float32)  6.9 us
  transfers between devices with their start and end apart: 4, of which 4 were waited for; matrix products, arithmetic and copies ran while one was open for 6% of the time, Pallas kernels for 0%

commit v1 on v0

--- a/solution.py
+++ b/solution.py
@@ -51,7 +51,9 @@
     run_total = total
     run_acc = acc
     keys = lax.all_gather(prefix_keys, "req", axis=0, tiled=True)
-    values = lax.all_gather(prefix_values, "req", axis=0, tiled=True)
+    values = jnp.concatenate(
+        lax.all_to_all(jnp.stack([prefix_values] * lax.axis_size("req")), "req", 0, 0), axis=0
+    )
     scores = jnp.einsum("sd,pd->sp", query, keys, preferred_element_type=jnp.float32) * scale
     new_top = jnp.maximum(top, jnp.max(scores, axis=-1))
     fade = jnp.exp(top - new_top)

time: 326 us -> 340 us (1.043)
  the two profiles are of different devices: /device:TPU:2 before, /device:TPU:4 now
where the time goes in v1:
time: 340 us
  blocking collectives  165 us (49%)
  waiting for transfers between devices  118 us (35%)
  matrix products  18.5 us (5%)
  between operations  13.9 us (4%)
  starting transfers between devices  10.5 us (3%)
  other arithmetic  9.71 us (3%)
  local copies, waits for them, and re-layouts  3.82 us (1%)
    all_gather x1, blocking collectives, on_device(): lax.all_gather(norm_gain, 'tp', axis=0, tiled=True)  165 us
    reduce_scatter x1, waiting for transfers between devices, on_device(): lax.psum_scatter(jnp.dot(context, w_out, preferred_element_type=jnp.float...  80 us
    all_gather x1, waiting for transfers between devices, on_device(): keys = lax.all_gather(prefix_keys, 'req', axis=0, tiled=True)  36.9 us
    all_to_all x1, starting transfers between devices, on_device(): lax.all_to_all(jnp.stack([prefix_values] * lax.axis_size('req')), 'req',...  10.4 us
    dot_general x1, matrix products, on_device(): jnp.dot(weights, values, preferred_element_type=jnp.float32)  6.91 us
  transfers between devices with their start and end apart: 4, of which 2 were waited for; matrix products, arithmetic and copies ran while one was open for 6% of the time, Pallas kernels for 0%

profile of v1, /device:TPU:4, one launch (start us, length us, event | category | flops | bytes accessed | tf_op | source)
XLA Modules:
  0.0 339.5 jit_solution(10793415863884733509)
XLA Ops:
  6.5 0.0 copy-start
  6.5 0.0 all-gather.4.cloned.1.call-start
  6.5 0.7 all-gather.4.cloned.1.call-update
  7.3 0.0 all-gather.6.cloned.1.call-start
  7.3 0.7 all-gather.6.cloned.1.call-update
  8.0 3.8 %stack.2 = bf16[32,512,128]{2,1,0:T(8,128)(2,1)} broadcast(bf16[512,128]{1,0:T(8,128)(2,1)} %param.16), dimensions={1,2} | broadcast | bytes 4325376 | tf_op jit(solution)/shard_map/stack | solution.py:55
  11.8 10.4 %all-to-all-start = ((bf16[32,512,128]{2,1,0:T(8,128)(2,1)}), bf16[32,512,128]{2,1,0:T(8,128)(2,1)}, u32[]{:S(2)}, u32[]{:S(2)}) async-start(bf16[32,512,128]{2,1,0:T(8,128)(2,1)} %stack.2), calls=%async_computation | async-start | bytes 8388608 | tf_op jit(solution)/shard_map/all_to_all | solution.py:55
  22.2 0.0 copy-start.3
  22.3 0.0 reduce-scatter.2.cloned.1.call-start
  22.3 0.0 copy-done.5
  22.3 164.8 %all-gather = bf16[16,1,256]{2,1,0:T(2,128)(2,1)S(1)} all-gather(bf16[1,1,256]{2,1,0:T(2,128)(2,1)S(1)} %reshape.56), channel_id=1, replica_groups=mesh['req'=32,'tp'=16] {'tp'}, dimensions={0}, use_global_device_ids=true | all-gather | bytes 8704 | tf_op jit(solution)/shard_map/all_gather | solution.py:23
  187.1 0.0 all-gather.4.cloned.1.call-done
  187.2 0.0 copy-start.1
  187.2 2.2 fusion
  189.4 0.0 copy-done.2
  189.4 0.0 copy-start.4
  189.5 2.6 fusion.34
  192.1 0.0 copy-done.3
  192.1 1.0 fusion.36
  193.1 0.3 fusion.21
  193.4 0.2 fusion.38
  193.7 0.1 convert_reduce_fusion.1
  193.8 0.9 convolution_convert_fusion.1
  194.6 36.9 %all-gather.6.cloned.1.call-done = bf16[16384,128]{1,0:T(8,128)(2,1)} async-done(((bf16[512,128]{1,0:T(8,128)(2,1)}), bf16[16384,128]{1,0:T(8,128)(2,1)}) %all-gather.6.cloned.1.call-update) | async-done | bytes 4194320 | tf_op jit(solution)/shard_map/all_gather | solution.py:53
  231.5 4.6 %fusion.39 = (f32[256]{0:T(256)S(1)}, f32[256,16384]{1,0:T(8,128)S(1)}) fusion(bf16[16384,128]{1,0:T(8,128)(2,1)} %all-gather.6.cloned.1.call-done, bf16[256,64]{0,1:T(8,128)(2,1)S(1)} %get-tuple-element.13, bf16[256,64]{0,1:T(8,128)(2,1)S(1)} %get-tuple-element.14), kind=kOutput, calls=%fused_computation.57 | convolution fusion | flops 1082261248 | bytes 21038080 | tf_op jit(solution)/shard_map/sd,pd->sp/dot_general | solution.py:57
  236.2 5.3 %convert_reduce_fusion = (f32[256]{0:T(256)S(1)}, bf16[256,16384]{1,0:T(8,128)(2,1)}) fusion(f32[256,16384]{1,0:T(8,128)S(1)} %get-tuple-element.18, f32[256]{0:T(256)S(1)} %max.13), kind=kLoop, calls=%fused_computation.1 | loop fusion | flops 16776960 | bytes 25167872 | tf_op jit(solution)/shard_map/reduce_sum | solution.py:61
  241.5 0.0 all-to-all-done
  241.5 6.9 %fusion.40 = f32[256,128]{1,0:T(8,128)S(1)} fusion(bf16[256,16384]{1,0:T(8,128)(2,1)} %get-tuple-element.8, bf16[16384,128]{1,0:T(8,128)(2,1)} %bitcast.4), kind=kOutput, calls=%fused_computation.58 | convolution fusion | flops 1073741824 | bytes 12713984 | tf_op jit(solution)/shard_map/dot_general | solution.py:62
  248.4 2.2 convolution_convert_fusion
  250.6 0.0 reduce-scatter.2.cloned.1.call-update
  251.3 80.0 %reduce-scatter.2.cloned.1.call-done = bf16[16,4096]{1,0:T(8,128)(2,1)} async-done(((bf16[256,4096]{1,0:T(8,128)(2,1)}), bf16[16,4096]{1,0:T(8,128)(2,1)}) %reduce-scatter.2.cloned.1.call-update) | async-done | bytes 131088 | tf_op jit(solution)/shard_map/reduce_scatter | solution.py:65
  331.3 1.6 fusion.7
  (13 shorter events, 0.1 us)
Async XLA Ops:
  6.5 241.9 %copy-start = (bf16[128,4096]{1,0:T(8,128)(2,1)S(1)}, bf16[128,4096]{1,0:T(8,128)(2,1)}, u32[]{:S(2)}) copy-start(bf16[128,4096]{1,0:T(8,128)(2,1)} %param.14) | copy-start | bytes 3145732
  6.5 180.6 %all-gather.4.cloned.1.call-start = ((), (), s32[]{:S(2)}) async-start(), calls=%async_computation.2 | async-start | bytes 2228224 | tf_op jit(solution)/shard_map/all_gather | solution.py:22
  7.3 224.2 %all-gather.6.cloned.1.call-start = ((), (), s32[]{:S(2)}) async-start(), calls=%async_computation.3 | async-start | bytes 4325376 | tf_op jit(solution)/shard_map/all_gather | solution.py:53
  11.8 10.5 %copy-start.5 = (bf16[256]{0:T(256)(128)(2,1)S(1)}, bf16[256]{0:T(256)(128)(2,1)}, u32[]{:S(2)}) copy-start(bf16[256]{0:T(256)(128)(2,1)} %param.10) | copy-start | bytes 1540
  11.8 177.6 %copy-start.2 = (bf16[4096,128]{1,0:T(8,128)(2,1)S(1)}, bf16[4096,128]{1,0:T(8,128)(2,1)}, u32[]{:S(2)}) copy-start(bf16[4096,128]{1,0:T(8,128)(2,1)} %param.12) | copy-start | bytes 3145732
  11.8 229.7 %all-to-all-start = ((bf16[32,512,128]{2,1,0:T(8,128)(2,1)}), bf16[32,512,128]{2,1,0:T(8,128)(2,1)}, u32[]{:S(2)}, u32[]{:S(2)}) async-start(bf16[32,512,128]{2,1,0:T(8,128)(2,1)} %stack.2), calls=%async_computation | async-start | bytes 8388608 | tf_op jit(solution)/shard_map/all_to_all | solution.py:55
  22.2 169.9 %copy-start.3 = (bf16[4096,128]{1,0:T(8,128)(2,1)S(1)}, bf16[4096,128]{1,0:T(8,128)(2,1)}, u32[]{:S(2)}) copy-start(bf16[4096,128]{1,0:T(8,128)(2,1)} %param.11) | copy-start | bytes 3145732
  22.3 309.1 %reduce-scatter.2.cloned.1.call-start = ((), (), s32[]{:S(2)}) async-start(), calls=%async_computation.4 | async-start | bytes 2228224 | tf_op jit(solution)/shard_map/reduce_scatter | solution.py:65
  187.2 4.9 %copy-start.1 = (bf16[1,256,4096]{2,1,0:T(8,128)(2,1)S(1)}, bf16[1,256,4096]{2,1,0:T(8,128)(2,1)}, u32[]{:S(2)}) copy-start(bf16[1,256,4096]{2,1,0:T(8,128)(2,1)} %all-gather.4.cloned.1.call-done) | copy-start | bytes 6291460
  189.4 4.3 %copy-start.4 = (bf16[4096,128]{1,0:T(8,128)(2,1)S(1)}, bf16[4096,128]{1,0:T(8,128)(2,1)}, u32[]{:S(2)}) copy-start(bf16[4096,128]{1,0:T(8,128)(2,1)} %param.13) | copy-start | bytes 3145732
Sparse Core Ops, SparseCore 0:
  9.3 154.1 all-gather.3
  166.6 64.8 all-gather.5
  250.8 80.5 reduce-scatter.1
